TPU v7x, 128 devices: a whole 4x4x4 slice. The times are simulated.
128 devices in a mesh: dp: 4 (over x_lo, core), tensor: 32 (over y, x_hi, z).
Axes of the slice: x: 4 (x_hi: 2, x_lo: 2; x = x_hi * 2 + x_lo), y: 4, z: 4, core: 2. Of those that a mesh axis runs over, the one named last changes fastest.
Arguments:
- qkv_master: float32 [7168, 21504], P(('dp', 'tensor')), may hold values from -0.0625 to 0.0625
- adapter_down: float32 [13, 7168, 128], P(None, ('dp', 'tensor')), may hold values from -0.0625 to 0.0625
- adapter_up: float32 [13, 128, 21504], P(None, None, 'tensor'), may hold values from -0.5 to 0.5
- adapter_pick: int32 [1], replicated, may hold values from 0 to 12
- out_master: float32 [3584, 7168], P(('dp', 'tensor')), may hold values from -0.0625 to 0.0625
- norm_gain: float32 [7168], replicated, may hold values from 0.1 to 1.9
- hidden_in: bfloat16 [2048, 3584], P(('dp', 'tensor')), may hold values from -6 to 6
- embed_in: bfloat16 [2048, 3584], P(('dp', 'tensor')), may hold values from -6 to 6
- prompt_len: int32 [4, 2], P('dp'), may hold values from 1 to 511, as said below
- prefix_len: int32 [4, 2], P('dp'), may hold values from 0 to 512, as said below
- prefix_holder: int32 [4, 2], P('dp'), may hold values from 0 to 3
- prefix_keys: bfloat16 [4, 512, 7168], P('dp', None, 'tensor'), may hold values from -6 to 6
- prefix_values: bfloat16 [4, 512, 7168], P('dp', None, 'tensor'), may hold values from -6 to 6
Outputs:
- server_qkv: bfloat16 [7168, 21504], P(None, 'tensor')
- server_out: bfloat16 [3584, 7168], P(None, 'tensor')
- block_out: bfloat16 [2048, 3584], P(('dp', 'tensor'))
- new_keys: bfloat16 [2048, 7168], P('dp', 'tensor')
- new_values: bfloat16 [2048, 7168], P('dp', 'tensor')
Inputs may be any that keep to these rules, and one draw needn't show every extreme that they name: `prompt_len`: the two prompt lengths of a replica add up to 512. `prefix_len`: exactly half of all requests extend a cached prefix (a positive length); the others have 0.
All inputs are finite; a program needn't handle non-finite values.
Results may differ from a plain program's by a relative error of at most 0.033.
Values may be sent and summed in bfloat16 or wider, within the bound.
A program may use at most 128 MiB of HBM per device.

v0:
```python
import math

import jax
import jax.numpy as jnp
from jax import lax
from jax.sharding import PartitionSpec as P


def partial_attention(queries, key_rows, value_rows, allowed, inv_scale):
    scores = (
        lax.dot_general(
            queries, key_rows, (((1,), (1,)), ((), ())), preferred_element_type=jnp.float32
        )
        * inv_scale
    )
    weights = jnp.where(allowed, jnp.exp(scores), jnp.float32(0.0))
    numerator = jnp.dot(
        weights.astype(jnp.bfloat16), value_rows, preferred_element_type=jnp.float32
    )
    return (numerator, jnp.sum(weights, axis=1))


def regroup_rows(columns, n_tensor, n_replica):
    col_count = columns.shape[1]
    row_count = columns.shape[0] // (n_tensor * n_replica)
    shaped = columns.reshape(n_tensor, n_replica, row_count, col_count)
    return jnp.transpose(shaped, (1, 0, 2, 3)).reshape(n_tensor * n_replica * row_count, col_count)


def body(
    qkv_master,
    adapter_down,
    adapter_up,
    adapter_pick,
    out_master,
    norm_gain,
    hidden_in,
    embed_in,
    prompt_len,
    prefix_len,
    prefix_holder,
    prefix_keys,
    prefix_values,
):
    n_tensor = lax.axis_size("tensor")
    n_replica = lax.axis_size("dp")
    chosen = adapter_pick[0]
    down_pick = lax.dynamic_index_in_dim(adapter_down, chosen, 0, keepdims=False).astype(
        jnp.bfloat16
    )
    up_pick = lax.dynamic_index_in_dim(adapter_up, chosen, 0, keepdims=False).astype(jnp.bfloat16)
    joined = jnp.concatenate([hidden_in, embed_in], axis=1).astype(jnp.float32)
    factor = lax.rsqrt(jnp.mean(joined * joined, axis=1, keepdims=True) + 1e-05)
    normed = (joined * factor * norm_gain).astype(jnp.bfloat16)
    all_rows, up_full = (
        lax.all_gather(normed, "tensor", axis=0, tiled=True),
        lax.all_gather(up_pick, "tensor", axis=1, tiled=True),
    )
    merged_qkv = (
        qkv_master + jnp.dot(down_pick, up_full, preferred_element_type=jnp.float32)
    ).astype(jnp.bfloat16)
    out_low = out_master.astype(jnp.bfloat16)
    rows_qkv, rows_out = (
        lax.all_gather(merged_qkv, "dp", axis=0, tiled=True),
        lax.all_gather(out_low, "dp", axis=0, tiled=True),
    )
    cols_qkv, cols_out = (
        lax.all_to_all(rows_qkv, "tensor", split_axis=1, concat_axis=0, tiled=True),
        lax.all_to_all(rows_out, "tensor", split_axis=1, concat_axis=0, tiled=True),
    )
    server_qkv = regroup_rows(cols_qkv, n_tensor, n_replica)
    server_out = regroup_rows(cols_out, n_tensor, n_replica)
    qkv_rows = jnp.dot(all_rows, server_qkv, preferred_element_type=jnp.float32).astype(
        jnp.bfloat16
    )
    head_size = qkv_rows.shape[1] // 3
    token_count = qkv_rows.shape[0]
    queries = qkv_rows[:, :head_size]
    new_keys = qkv_rows[:, head_size : 2 * head_size]
    new_values = qkv_rows[:, 2 * head_size :]
    inv_scale = 1.0 / math.sqrt(head_size)
    positions = jnp.arange(token_count, dtype=jnp.int32)
    lengths = prompt_len[0]
    request = (positions >= lengths[0]).astype(jnp.int32)
    block_rows = math.gcd(token_count, 512)
    first_row = 0
    last_row = first_row + block_rows
    allowed = (request[first_row:last_row, None] == request[None, :]) & (
        positions[None, :] <= positions[first_row:last_row, None]
    )
    numerator, weight_sum = partial_attention(queries, new_keys, new_values, allowed, inv_scale)
    own_parts = numerator
    own_sums = weight_sum
    cached_len = prefix_len[0]
    holders = prefix_holder[0]
    row_holder = jnp.where(request == 1, holders[1], holders[0])
    row_limit = jnp.where(request == 1, cached_len[1], cached_len[0])
    slot_ids = jnp.arange(prefix_keys.shape[1], dtype=jnp.int32)
    offset = jnp.int32(0)
    numerator = own_parts
    weight_sum = own_sums
    key_piece = lax.all_gather(prefix_keys, "dp", axis=0, tiled=True)
    value_piece = lax.all_gather(prefix_values, "dp", axis=0, tiled=True)
    for member in range(key_piece.shape[0]):
        replica = offset + member
        first_row = 0
        last_row = first_row + block_rows
        usable = (row_holder[first_row:last_row, None] == replica) & (
            slot_ids[None, :] < row_limit[first_row:last_row, None]
        )
        part_num, part_sum = partial_attention(
            queries, key_piece[member], value_piece[member], usable, inv_scale
        )
        numerator = numerator + part_num
        weight_sum = weight_sum + part_sum
    numerator, weight_sum = (numerator, weight_sum)
    attention = (numerator / weight_sum[:, None]).astype(jnp.bfloat16)
    block_out = lax.psum_scatter(
        lax.dot_general(
            attention, server_out, (((1,), (1,)), ((), ())), preferred_element_type=jnp.float32
        ).astype(jnp.bfloat16),
        "tensor",
        scatter_dimension=0,
        tiled=True,
    )
    return (server_qkv, server_out, block_out, new_keys, new_values)


def solution(mesh):
    in_specs = (
        P(("dp", "tensor"), None),
        P(None, ("dp", "tensor"), None),
        P(None, None, "tensor"),
        P(),
        P(("dp", "tensor"), None),
        P(),
        P(("dp", "tensor"), None),
        P(("dp", "tensor"), None),
        P("dp", None),
        P("dp", None),
        P("dp", None),
        P("dp", None, "tensor"),
        P("dp", None, "tensor"),
    )
    out_specs = (
        P(None, "tensor"),
        P(None, "tensor"),
        P(("dp", "tensor"), None),
        P("dp", "tensor"),
        P("dp", "tensor"),
    )
    return jax.shard_map(body, mesh=mesh, in_specs=in_specs, out_specs=out_specs, check_vma=False)
```

profile of v0, /device:TPU:0, one launch (start us, length us, event | category | flops | bytes accessed | tf_op | source)
XLA Modules:
  0.0 744.3 jit_solution(5909597050961547122)
XLA Ops:
  7.2 0.0 copy-start
  7.2 0.0 all-gather.11.cloned.1.call-start
  7.9 1.7 dynamic-slice_convert_fusion
  9.6 0.0 all-gather.11.cloned.1.call-update
  9.6 0.0 all-gather.13.cloned.1.call-start
  9.7 2.0 convert_bitcast_fusion
  11.7 0.0 all-gather.13.cloned.1.call-update
  11.7 0.0 copy-start.4
  11.7 0.0 copy-start.5
  11.7 0.0 copy-start.9
  11.7 0.0 all-gather.7.cloned.1.call-start
  11.8 90.2 %all-gather.11.cloned.1.call-done = bf16[1,128,21504]{1,2,0:T(8,128)(2,1)} async-done(((bf16[1,128,672]{1,2,0:T(8,128)(2,1)}), bf16[1,128,21504]{1,2,0:T(8,128)(2,1)}) %all-gather.11.cloned.1.call-update) | async-done | bytes 5505040 | tf_op jit(solution)/shard_map/all_gather | solution.py:57
  101.9 0.0 copy-done
  101.9 8.7 %fusion = bf16[56,21504]{1,0:T(8,128)(2,1)} fusion(f32[56,21504]{1,0:T(8,128)} %param.13, bf16[1,128,21504]{1,2,0:T(8,128)(2,1)} %all-gather.11.cloned.1.call-done, f32[13,56,128]{2,1,0:T(8,128)S(1)} %copy-done, s32[]{:T(128)S(6)} %select_n.46), kind=kOutput, calls=%fused_computation.1 | convolution fusion | flops 310689792 | bytes 12744708 | tf_op jit(solution)/shard_map/dot_general | solution.py:60
  110.7 0.0 all-gather.7.cloned.1.call-update
  110.7 0.0 all-gather.9.cloned.1.call-start
  110.7 0.0 copy-done.4
  110.7 0.0 copy-done.5
  110.8 0.2 fusion.26
  111.0 0.8 fusion.28
  111.8 0.0 all-gather.9.cloned.1.call-update
  111.8 17.1 %all-gather.13.cloned.1.call-done = bf16[4,28,7168]{2,1,0:T(8,128)(2,1)} async-done(((bf16[1,28,7168]{2,1,0:T(8,128)(2,1)}), bf16[4,28,7168]{2,1,0:T(8,128)(2,1)}) %all-gather.13.cloned.1.call-update) | async-done | bytes 1605648 | tf_op jit(solution)/shard_map/all_gather | solution.py:65
  128.9 3.7 all_to_all.27
  132.6 2.3 copy.29
  134.9 9.4 %all-to-all-start.1 = ((bf16[112,32,224]{2,0,1:T(8,128)(2,1)}), bf16[112,32,224]{2,0,1:T(8,128)(2,1)S(1)}, u32[]{:S(2)}, u32[]{:S(2)}) async-start(bf16[112,32,224]{2,0,1:T(8,128)(2,1)} %copy.29), calls=%async_computation.1 | async-start | bytes 3670016 | tf_op jit(solution)/shard_map/all_to_all | solution.py:69
  144.3 97.9 %all-gather.7.cloned.1.call-done = bf16[224,21504]{1,0:T(8,128)(2,1)} async-done(((bf16[56,21504]{1,0:T(8,128)(2,1)}), bf16[224,21504]{1,0:T(8,128)(2,1)}) %all-gather.7.cloned.1.call-update) | async-done | bytes 9633808 | tf_op jit(solution)/shard_map/all_gather | solution.py:64
  242.2 20.8 %all_to_all.24 = bf16[224,32,672]{2,1,0:T(8,128)(2,1)} reshape(bf16[224,21504]{1,0:T(8,128)(2,1)} %all-gather.7.cloned.1.call-done) | data formatting | bytes 19267584 | tf_op jit(solution)/shard_map/all_to_all | solution.py:68
  263.1 11.6 %copy.27 = bf16[224,32,672]{2,0,1:T(8,128)(2,1)} copy(bf16[224,32,672]{2,1,0:T(8,128)(2,1)} %all_to_all.24) | data formatting | bytes 19267584 | tf_op jit(solution)/shard_map/all_to_all | solution.py:68
  274.7 0.0 copy-start.8
  274.7 0.0 all-to-all-done.1
  274.8 10.4 %all-to-all-start = ((bf16[224,32,672]{2,0,1:T(8,128)(2,1)}), bf16[224,32,672]{2,0,1:T(8,128)(2,1)}, u32[]{:S(2)}, u32[]{:S(2)}) async-start(bf16[224,32,672]{2,0,1:T(8,128)(2,1)} %copy.27), calls=%async_computation | async-start | bytes 22020096 | tf_op jit(solution)/shard_map/all_to_all | solution.py:68
  285.2 0.0 reduce-scatter.2.cloned.1.call-start
  285.2 0.6 fusion.40
  285.8 0.0 copy-done.10
  285.8 1.3 select_compare_fusion
  287.1 1.3 select_compare_fusion.2
  288.5 0.0 copy-done.12
  288.5 0.6 fusion.41
  289.1 1.3 broadcast_select_fusion
  290.4 194.6 %all_gather.22 = bf16[4,512,224]{1,2,0:T(8,128)(2,1)} all-gather(bf16[1,512,224]{1,2,0:T(8,128)(2,1)S(1)} %copy-done.7), channel_id=1, replica_groups=mesh['dp'=4,'tensor'=32] {'dp'}, dimensions={0}, use_global_device_ids=true | all-gather | bytes 1146880 | tf_op jit(solution)/shard_map/all_gather | solution.py:102
  485.0 11.8 %all_gather.23 = bf16[4,512,224]{1,2,0:T(8,128)(2,1)S(1)} all-gather(bf16[1,512,224]{1,2,0:T(8,128)(2,1)S(1)} %copy-done.8), channel_id=1, replica_groups=mesh['dp'=4,'tensor'=32] {'dp'}, dimensions={0}, use_global_device_ids=true | all-gather | bytes 1146880 | tf_op jit(solution)/shard_map/all_gather | solution.py:103
  496.8 0.7 copy.30
  497.4 2.4 copy.31
  499.8 2.8 reshape.99
  502.6 0.0 all-to-all-done
  502.6 9.8 %copy.28 = bf16[4,32,56,672]{3,2,1,0:T(8,128)(2,1)} copy(bf16[4,32,56,672]{3,2,0,1:T(8,128)(2,1)} %bitcast.5) | data formatting | bytes 19267584 | tf_op jit(solution)/shard_map/transpose | solution.py:27
  512.5 13.6 %convolution_convert_fusion.1 = bf16[512,672]{0,1:T(8,128)(2,1)S(1)} fusion(bf16[512,7168]{1,0:T(8,128)(2,1)} %all-gather.9.cloned.1.call-done, bf16[7168,672]{1,0:T(8,128)(2,1)} %bitcast.72), kind=kOutput, calls=%fused_computation.19 | convolution fusion | flops 4932845568 | bytes 17661952 | tf_op jit(solution)/shard_map/dot_general | solution.py:73
  526.1 0.0 copy-start.6
  526.1 0.0 copy-start.2
  526.1 1.3 fusion.42
  527.5 0.5 fusion.43
  528.0 0.5 fusion.44
  528.5 0.5 fusion.46
  529.1 0.5 fusion.45
  529.5 0.0 copy-done.2
  529.5 0.3 fusion.24
  529.8 0.3 convolution_add_fusion.4
  530.1 0.3 convolution_add_fusion.3
  530.4 1.1 convolution_add_fusion.2
  531.5 4.6 convolution_convert_fusion
  536.0 0.0 reduce-scatter.2.cloned.1.call-update
  536.1 2.5 copy.33
  538.6 13.5 %copy.32 = bf16[7168,672]{0,1:T(8,128)(2,1)} copy(bf16[7168,672]{1,0:T(8,128)(2,1)} %bitcast.73) | data formatting | bytes 19267584
  552.0 185.8 %reduce-scatter.2.cloned.1.call-done = bf16[16,3584]{1,0:T(8,128)(2,1)} async-done(((bf16[512,3584]{1,0:T(8,128)(2,1)}), bf16[16,3584]{1,0:T(8,128)(2,1)}) %reduce-scatter.2.cloned.1.call-update) | async-done | bytes 114704 | tf_op jit(solution)/shard_map/reduce_scatter | solution.py:118
  (18 shorter events, 0.1 us)
Async XLA Ops:
  7.2 94.8 %copy-start = (f32[13,56,128]{2,1,0:T(8,128)S(1)}, f32[13,56,128]{2,1,0:T(8,128)}, u32[]{:S(2)}) copy-start(f32[13,56,128]{2,1,0:T(8,128)} %param.14) | copy-start | bytes 1118212
  7.2 94.7 %all-gather.11.cloned.1.call-start = ((), (), s32[]{:S(2)}) async-start(), calls=%async_computation.6 | async-start | bytes 5677056 | tf_op jit(solution)/shard_map/all_gather | solution.py:57
  9.6 119.3 %all-gather.13.cloned.1.call-start = ((), (), s32[]{:S(2)}) async-start(), calls=%async_computation.7 | async-start | bytes 2293760 | tf_op jit(solution)/shard_map/all_gather | solution.py:65
  11.7 99.1 %copy-start.4 = (bf16[16,3584]{1,0:T(8,128)(2,1)S(1)}, bf16[16,3584]{1,0:T(8,128)(2,1)}, u32[]{:S(2)}) copy-start(bf16[16,3584]{1,0:T(8,128)(2,1)} %param.20) | copy-start | bytes 344068
  11.7 99.1 %copy-start.5 = (bf16[16,3584]{1,0:T(8,128)(2,1)S(1)}, bf16[16,3584]{1,0:T(8,128)(2,1)}, u32[]{:S(2)}) copy-start(bf16[16,3584]{1,0:T(8,128)(2,1)} %param.19) | copy-start | bytes 344068
  11.7 99.2 %copy-start.9 = (f32[7168]{0:T(1024)S(1)}, f32[7168]{0:T(1024)}, u32[]{:S(2)}) copy-start(f32[7168]{0:T(1024)} %param.18) | copy-start | bytes 86020
  11.7 230.5 %all-gather.7.cloned.1.call-start = ((), (), s32[]{:S(2)}) async-start(), calls=%async_computation.3 | async-start | bytes 12042240 | tf_op jit(solution)/shard_map/all_gather | solution.py:64
  110.7 401.8 %all-gather.9.cloned.1.call-start = ((), (), s32[]{:S(2)}) async-start(), calls=%async_computation.4 | async-start | bytes 7569408 | tf_op jit(solution)/shard_map/all_gather | solution.py:56
  134.9 139.8 %all-to-all-start.1 = ((bf16[112,32,224]{2,0,1:T(8,128)(2,1)}), bf16[112,32,224]{2,0,1:T(8,128)(2,1)S(1)}, u32[]{:S(2)}, u32[]{:S(2)}) async-start(bf16[112,32,224]{2,0,1:T(8,128)(2,1)} %copy.29), calls=%async_computation.1 | async-start | bytes 3670016 | tf_op jit(solution)/shard_map/all_to_all | solution.py:69
  274.7 10.5 %copy-start.11 = (s32[1,2]{1,0:T(1,128)S(1)}, s32[1,2]{1,0:T(1,128)}, u32[]{:S(2)}) copy-start(s32[1,2]{1,0:T(1,128)} %param.23) | copy-start | bytes 28
  274.7 11.1 %copy-start.10 = (s32[1,2]{1,0:T(1,128)S(1)}, s32[1,2]{1,0:T(1,128)}, u32[]{:S(2)}) copy-start(s32[1,2]{1,0:T(1,128)} %param.21) | copy-start | bytes 28
  274.7 13.8 %copy-start.12 = (s32[1,2]{1,0:T(1,128)S(1)}, s32[1,2]{1,0:T(1,128)}, u32[]{:S(2)}) copy-start(s32[1,2]{1,0:T(1,128)} %param.22) | copy-start | bytes 28
  274.7 15.7 %copy-start.7 = (bf16[1,512,224]{1,2,0:T(8,128)(2,1)S(1)}, bf16[1,512,224]{1,2,0:T(8,128)(2,1)}, u32[]{:S(2)}) copy-start(bf16[1,512,224]{1,2,0:T(8,128)(2,1)} %param.24) | copy-start | bytes 688132
  274.7 210.2 %copy-start.8 = (bf16[1,512,224]{1,2,0:T(8,128)(2,1)S(1)}, bf16[1,512,224]{1,2,0:T(8,128)(2,1)}, u32[]{:S(2)}) copy-start(bf16[1,512,224]{1,2,0:T(8,128)(2,1)} %param.25) | copy-start | bytes 688132
  274.8 227.9 %all-to-all-start = ((bf16[224,32,672]{2,0,1:T(8,128)(2,1)}), bf16[224,32,672]{2,0,1:T(8,128)(2,1)}, u32[]{:S(2)}, u32[]{:S(2)}) async-start(bf16[224,32,672]{2,0,1:T(8,128)(2,1)} %copy.27), calls=%async_computation | async-start | bytes 22020096 | tf_op jit(solution)/shard_map/all_to_all | solution.py:68
  285.2 452.6 %reduce-scatter.2.cloned.1.call-start = ((), (), s32[]{:S(2)}) async-start(), calls=%async_computation.5 | async-start | bytes 3784704 | tf_op jit(solution)/shard_map/reduce_scatter | solution.py:118
  512.5 13.6 %copy-start.3 = (bf16[4,512,224]{1,2,0:T(8,128)(2,1)S(1)}, bf16[4,512,224]{1,2,0:T(8,128)(2,1)}, u32[]{:S(2)}) copy-start(bf16[4,512,224]{1,2,0:T(8,128)(2,1)} %all_gather.22) | copy-start | bytes 2752516
  526.1 3.0 copy-start.6
  526.1 3.4 copy-start.2
  538.6 199.3 %copy-start.1 = (f32[13,56,128]{2,1,0:T(8,128)S(1)}, f32[13,56,128]{2,1,0:T(8,128)}, u32[]{:S(2)}) copy-start(f32[13,56,128]{2,1,0:T(8,128)} %param.14) | copy-start | bytes 1118212
Sparse Core Ops, SparseCore 0:
  11.6 90.2 all-gather.10
  104.2 24.7 all-gather.12
  131.2 111.0 all-gather.6
  245.7 228.1 all-gather.8
  536.2 201.5 reduce-scatter.1
where the time goes:
time: 746 us; the launch traced here: 744 us
  waiting for transfers between devices  391 us (52%)
  blocking collectives  206 us (28%)
  local copies, waits for them, and re-layouts  73 us (10%)
  matrix products  32.2 us (4%)
  starting transfers between devices  20 us (3%)
  between operations  14.7 us (2%)
    all_gather x1, blocking collectives, body(): key_piece = lax.all_gather(prefix_keys, 'dp', axis=0, tiled=True)  195 us
    reduce_scatter x1, waiting for transfers between devices, body(): lax.psum_scatter(lax.dot_general(attention, server_out, (((1,), (1,)), ((...  186 us
    all_gather x1, waiting for transfers between devices, body(): lax.all_gather(merged_qkv, 'dp', axis=0, tiled=True)  97.9 us
    all_gather x1, waiting for transfers between devices, body(): lax.all_gather(up_pick, 'tensor', axis=1, tiled=True)  90.2 us
    all_to_all x2, local copies, waits for them, and re-layouts, body(): lax.all_to_all(rows_qkv, 'tensor', split_axis=1, concat_axis=0, tiled=True)  32.5 us
    all_gather x1, waiting for transfers between devices, body(): lax.all_gather(out_low, 'dp', axis=0, tiled=True)  17.1 us
    unnamed x28, local copies, waits for them, and re-layouts  16 us
  transfers between devices with their start and end apart: 7, of which 4 were waited for; matrix products, arithmetic and copies ran while one was open for 8% of the time, Pallas kernels for 0%

commit v1 on v0

v1 whole, which is shorter than its diff:
```python
import functools
import math

import jax
import jax.numpy as jnp
from jax import lax
from jax.experimental import pallas as pl
from jax.experimental.pallas import tpu as pltpu
from jax.sharding import PartitionSpec as P

MESH = pl.DeviceIdType.MESH
N_Y, N_XH, N_Z = 4, 2, 4


def position():
    dp = lax.axis_index("dp")
    t = lax.axis_index("tensor")
    xl, c = lax.div(dp, 2), lax.rem(dp, 2)
    y, xh, z = lax.div(t, 8), lax.rem(lax.div(t, 4), 2), lax.rem(t, 4)
    return dp, t, xl, c, y, xh, z


def tensor_of(y, xh, z):
    return y * 8 + xh * 4 + z


def pack_kernel(master_ref, out_ref, down_ref, a_ref, b_ref):
    rows, width = master_ref.shape
    out_rows, out_width = out_ref.shape
    cols, out_cols = width // 4, out_width // 4
    whole = cols // 128 * 128
    master = master_ref[...].astype(jnp.bfloat16).astype(jnp.float32)
    outs = out_ref[...]
    down = down_ref[...].astype(jnp.bfloat16)
    for k in range(4):
        a_ref[k, :, 0:cols] = master[:, k * cols : (k + 1) * cols].astype(jnp.bfloat16)
        piece = outs[:, k * out_cols : (k + 1) * out_cols]
        a_ref[k, 0:out_rows, cols:768] = piece[:, 128:].astype(jnp.bfloat16)
        a_ref[k, out_rows:, cols:768] = jnp.zeros((rows - out_rows, 768 - cols), jnp.bfloat16)
        b_ref[k, 0:rows, :] = down
        b_ref[k, rows : rows + 32, :] = jnp.concatenate(
            [piece[:, :128], jnp.zeros((32 - out_rows, 128), jnp.float32)], axis=0
        ).astype(jnp.bfloat16)


def pack(master, outs, down):
    rows, out_rows = master.shape[0], outs.shape[0]
    n = 8
    return pl.pallas_call(
        pack_kernel,
        grid=(n,),
        in_specs=[
            pl.BlockSpec((rows, master.shape[1] // n), lambda i: (0, i)),
            pl.BlockSpec((out_rows, outs.shape[1] // n), lambda i: (0, i)),
            pl.BlockSpec(down.shape, lambda i: (0, 0)),
        ],
        out_specs=[
            pl.BlockSpec((4, rows, 768), lambda i: (i, 0, 0)),
            pl.BlockSpec((4, rows + 32, 128), lambda i: (i, 0, 0)),
        ],
        out_shape=[
            jax.ShapeDtypeStruct((32, rows, 768), jnp.bfloat16),
            jax.ShapeDtypeStruct((32, rows + 32, 128), jnp.bfloat16),
        ],
    )(master, outs, down)


def exchange_kernel(
    sa, sb, na, nb, pk, pv,
    ra, rb, xa, xb, gk, gv,
    w_send, w_recv, n_send, n_recv, s_send, s_recv, f_send, f_recv,
    t_send, t_recv, p_send, p_recv, l_sem,
):
    dp, t, xl, c, y, xh, z = position()
    near = (1 - xl) * 2 + c
    core = xl * 2 + (1 - c)
    me = dp * 32 + t

    def remote(src, dst, send, recv, to_dp, to_t):
        return pltpu.make_async_remote_copy(
            src_ref=src, dst_ref=dst, send_sem=send, recv_sem=recv,
            device_id=(to_dp, to_t), device_id_type=MESH,
        )

    own = [
        pltpu.make_async_copy(na, xa.at[y * 2 + xh, z], l_sem.at[0]),
        pltpu.make_async_copy(nb, xb.at[y * 2 + xh, z], l_sem.at[1]),
        pltpu.make_async_copy(sa.at[t], ra.at[me], l_sem.at[2]),
        pltpu.make_async_copy(sb.at[t], rb.at[me], l_sem.at[3]),
        pltpu.make_async_copy(pk, gk.at[dp], l_sem.at[4]),
        pltpu.make_async_copy(pv, gv.at[dp], l_sem.at[5]),
    ]
    for copy in own:
        copy.start()

    other = tensor_of(y, 1 - xh, z)
    step1 = [
        remote(na, xa.at[y * 2 + xh, z], t_send.at[0], t_recv.at[0], dp, other),
        remote(nb, xb.at[y * 2 + xh, z], t_send.at[1], t_recv.at[1], dp, other),
    ]
    for copy in step1:
        copy.start()

    prefix = []
    for i, (src, dst) in enumerate(((pk, gk), (pv, gv))):
        prefix.append(remote(src, dst.at[dp], p_send.at[i], p_recv.at[i], near, t))
        prefix.append(remote(src, dst.at[dp], p_send.at[2 + i], p_recv.at[2 + i], core, t))
    for copy in prefix:
        copy.start()

    def chunk(i, which, sign):
        a, s, b = lax.div(i, 8), lax.rem(lax.div(i, 4), 2), lax.rem(i, 4)
        to_dp = lax.rem(xl + s, 2) * 2 + c
        to_t = tensor_of(lax.rem(y + a, 4), lax.rem(xh + s, 2), lax.rem(z + b, 4))
        src, dst = ((sa, ra), (sb, rb))[which]
        return remote(
            src.at[to_t], dst.at[me], w_send.at[which, i], w_recv.at[which, i], to_dp, to_t
        )

    def send_chunk(i, carry):
        chunk(i, 0, 1).start()
        chunk(i, 1, 1).start()
        return carry

    lax.fori_loop(1, 32, send_chunk, 0)

    for copy in step1:
        copy.wait_recv()
    own[0].wait()
    own[1].wait()
    step2 = []
    for d in range(1, 4):
        to_z = tensor_of(y, xh, lax.rem(z + d, 4))
        to_y = tensor_of(lax.rem(y + d, 4), xh, z)
        mine = pl.ds(y * 2, 2)
        step2.append(
            remote(xa.at[mine, z], xa.at[mine, z], t_send.at[1 + d], t_recv.at[1 + d], dp, to_z)
        )
        step2.append(
            remote(xb.at[mine, z], xb.at[mine, z], t_send.at[4 + d], t_recv.at[4 + d], dp, to_y)
        )
    for copy in step2:
        copy.start()

    own[2].wait()
    own[3].wait()

    def first_of(j, from_xl):
        a, s = lax.div(j, 2), lax.rem(j, 2)
        src_dp = lax.rem(from_xl + s, 2) * 2
        return src_dp * 32 + tensor_of(lax.rem(y + 4 - a, 4), lax.rem(xh + s, 2), 0)

    def group(j, which, send, recv, to_dp, from_xl, from_c):
        g = first_of(j, from_xl) + from_c * 32
        ref = (ra, rb)[which].at[pl.ds(g, 4)]
        return remote(ref, ref, send.at[which, j], recv.at[which, j], to_dp, t)

    def forward(j, carry):
        for which in range(2):
            for b in range(4):
                i = j * 4 + b

                @pl.when(i > 0)
                def _():
                    chunk(i, which, 1).wait_recv()

            group(j, which, n_send, n_recv, near, xl, c).start()
            group(j, which, s_send, s_recv, core, xl, c).start()
        return carry

    lax.fori_loop(0, 4, forward, 0)

    for copy in step2:
        copy.wait_recv()
    step3 = []
    for k, d in enumerate((1, 3)):
        to_y = tensor_of(lax.rem(y + d, 4), xh, z)
        to_z = tensor_of(y, xh, lax.rem(z + d, 4))
        for h in range(2):
            rows = pl.ds(y * 2 + h, 1)
            step3.append(
                remote(
                    xa.at[rows], xa.at[rows],
                    t_send.at[8 + k * 2 + h], t_recv.at[8 + k * 2 + h], dp, to_y,
                )
            )
            rows = pl.ds(h * 4, 4)
            step3.append(
                remote(
                    xb.at[rows, z], xb.at[rows, z],
                    t_send.at[12 + k * 2 + h], t_recv.at[12 + k * 2 + h], dp, to_z,
                )
            )
    for copy in step3:
        copy.start()

    lax.fori_loop(4, 8, forward, 0)

    late = []
    for i, dst in enumerate((gk, gv)):
        prefix[2 * i].wait_recv()
        late.append(
            remote(dst.at[near], dst.at[near], p_send.at[4 + i], p_recv.at[4 + i], core, t)
        )
        late[-1].start()

    for copy in step3:
        copy.wait_recv()
    step4 = []
    for h, d in ((0, 1), (1, 3)):
        src_y, src_z = lax.rem(y + 4 - d, 4), lax.rem(z + 4 - d, 4)
        to_y = tensor_of(lax.rem(y + d, 4), xh, z)
        to_z = tensor_of(y, xh, lax.rem(z + d, 4))
        rows = pl.ds(src_y * 2 + h, 1)
        step4.append(
            remote(xa.at[rows], xa.at[rows], t_send.at[16 + h], t_recv.at[16 + h], dp, to_y)
        )
        rows = pl.ds(h * 4, 4)
        step4.append(
            remote(
                xb.at[rows, src_z], xb.at[rows, src_z],
                t_send.at[18 + h], t_recv.at[18 + h], dp, to_z,
            )
        )
    for copy in step4:
        copy.start()

    def pass_on(j, carry):
        for which in range(2):
            group(j, which, n_send, n_recv, near, xl, c).wait_recv()
            group(j, which, f_send, f_recv, core, 1 - xl, c).start()
        return carry

    lax.fori_loop(0, 8, pass_on, 0)

    def finish(j, carry):
        for which in range(2):
            group(j, which, s_send, s_recv, core, xl, c).wait_recv()
            group(j, which, f_send, f_recv, core, 1 - xl, c).wait()
            group(j, which, n_send, n_recv, near, xl, c).wait_send()
            group(j, which, s_send, s_recv, core, xl, c).wait_send()
        return carry

    lax.fori_loop(0, 8, finish, 0)

    def sent(i, carry):
        chunk(i, 0, 1).wait_send()
        chunk(i, 1, 1).wait_send()
        return carry

    lax.fori_loop(1, 32, sent, 0)
    for copy in step4:
        copy.wait_recv()
    for copy in step1 + step2 + step3 + step4:
        copy.wait_send()
    own[4].wait()
    own[5].wait()
    for i in range(2):
        prefix[2 * i + 1].wait_recv()
    for copy in prefix:
        copy.wait_send()
    for copy in late:
        copy.wait()


def exchange(sa, sb, na, nb, pk, pv):
    half = na.shape[1]
    any_spec = pl.BlockSpec(memory_space=pl.ANY)
    bf16 = jnp.bfloat16
    dma = pltpu.SemaphoreType.DMA
    return pl.pallas_call(
        exchange_kernel,
        in_specs=[any_spec] * 6,
        out_specs=[any_spec] * 6,
        out_shape=[
            jax.ShapeDtypeStruct((128,) + sa.shape[1:], bf16),
            jax.ShapeDtypeStruct((128,) + sb.shape[1:], bf16),
            jax.ShapeDtypeStruct((8, 4, 16, half), bf16),
            jax.ShapeDtypeStruct((8, 4, 16, half), bf16),
            jax.ShapeDtypeStruct((4,) + pk.shape, bf16),
            jax.ShapeDtypeStruct((4,) + pv.shape, bf16),
        ],
        scratch_shapes=[
            dma((2, 32)), dma((2, 32)),
            dma((2, 8)), dma((2, 8)),
            dma((2, 8)), dma((2, 8)),
            dma((2, 8)), dma((2, 8)),
            dma((20,)), dma((20,)),
            dma((6,)), dma((6,)),
            dma((6,)),
        ],
        compiler_params=pltpu.CompilerParams(has_side_effects=True),
        name="exchange",
    )(sa, sb, na, nb, pk, pv)


def project_kernel(
    attn, weights, out,
    pa, pb, ra1, rb1, qa, qb, ra2, rb2, ha, hb, ra3, rb3,
    send, recv,
):
    dp, t, xl, c, y, xh, z = position()
    half = pa.shape[-1]
    step = 256

    def remote(src, dst, k, to_t):
        return pltpu.make_async_remote_copy(
            src_ref=src, dst_ref=dst, send_sem=send.at[k], recv_sem=recv.at[k],
            device_id=(dp, to_t), device_id_type=MESH,
        )

    def fill(dst, first):
        for f in range(half // step):
            block = lax.dot_general(
                attn[...],
                weights[first + f * step : first + (f + 1) * step, :],
                (((1,), (1,)), ((), ())),
                preferred_element_type=jnp.float32,
            )
            dst[:, :, :, f * step : (f + 1) * step] = block.astype(jnp.bfloat16).reshape(
                8, 4, 16, step
            )

    def f32(x):
        return x.astype(jnp.float32)

    fill(pa, 0)
    a1, b1, a2, b2 = [], [], [], []
    for d in range(1, 4):
        to = lax.rem(z + d, 4)
        a1.append(remote(pa.at[:, to], ra1.at[d - 1], d - 1, tensor_of(y, xh, to)))
        a1[-1].start()
    fill(pb, half)
    for d in range(1, 4):
        to = lax.rem(y + d, 4)
        b1.append(remote(pb.at[pl.ds(to * 2, 2)], rb1.at[d - 1], 2 + d, tensor_of(to, xh, z)))
        b1[-1].start()

    for copy in a1:
        copy.wait_recv()
    for i in range(8):
        total = f32(pa[i, z]) + f32(ra1[0, i]) + f32(ra1[1, i]) + f32(ra1[2, i])
        qa[i] = total.astype(jnp.bfloat16)
    for d in range(1, 4):
        to = lax.rem(y + d, 4)
        a2.append(remote(qa.at[pl.ds(to * 2, 2)], ra2.at[d - 1], 5 + d, tensor_of(to, xh, z)))
        a2[-1].start()
    for copy in b1:
        copy.wait_recv()
    for h in range(2):
        for i in range(4):
            total = f32(pb[y * 2 + h, i]) + f32(rb1[0, h, i]) + f32(rb1[1, h, i])
            qb[h, i] = (total + f32(rb1[2, h, i])).astype(jnp.bfloat16)
    for d in range(1, 4):
        to = lax.rem(z + d, 4)
        b2.append(remote(qb.at[:, to], rb2.at[d - 1], 8 + d, tensor_of(y, xh, to)))
        b2[-1].start()

    partner = tensor_of(y, 1 - xh, z)
    for copy in a2:
        copy.wait_recv()
    for h in range(2):
        total = f32(qa[y * 2 + h]) + f32(ra2[0, h]) + f32(ra2[1, h]) + f32(ra2[2, h])
        ha[h] = total.astype(jnp.bfloat16)
    a3 = remote(ha.at[1 - xh], ra3, 12, partner)
    a3.start()
    for copy in b2:
        copy.wait_recv()
    for h in range(2):
        total = f32(qb[h, z]) + f32(rb2[0, h]) + f32(rb2[1, h]) + f32(rb2[2, h])
        hb[h] = total.astype(jnp.bfloat16)
    b3 = remote(hb.at[1 - xh], rb3, 13, partner)
    b3.start()
    a3.wait_recv()
    out[:, :half] = (f32(ha[xh]) + f32(ra3[...])).astype(jnp.bfloat16)
    b3.wait_recv()
    out[:, half:] = (f32(hb[xh]) + f32(rb3[...])).astype(jnp.bfloat16)
    for copy in a1 + b1 + a2 + b2 + [a3, b3]:
        copy.wait_send()


def project(attn, weights):
    features = weights.shape[0]
    half = features // 2
    vmem = pl.BlockSpec(memory_space=pltpu.VMEM)

    def room(*shape):
        return pltpu.VMEM(shape + (16, half), jnp.bfloat16)

    return pl.pallas_call(
        project_kernel,
        in_specs=[vmem] * 2,
        out_specs=vmem,
        out_shape=jax.ShapeDtypeStruct((16, features), jnp.bfloat16),
        scratch_shapes=[
            room(8, 4), room(8, 4),
            room(3, 8), room(3, 2, 4),
            room(8), room(2, 4),
            room(3, 2), room(3, 2),
            room(2), room(2),
            room(), room(),
            pltpu.SemaphoreType.DMA((14,)),
            pltpu.SemaphoreType.DMA((14,)),
        ],
        compiler_params=pltpu.CompilerParams(
            has_side_effects=True, vmem_limit_bytes=40 * 1024 * 1024
        ),
        name="project",
    )(attn, weights)


def partial_attention(queries, key_cols, value_cols, allowed, inv_scale):
    scores = jnp.dot(queries, key_cols, preferred_element_type=jnp.float32) * inv_scale
    weights = jnp.where(allowed, jnp.exp(scores), jnp.float32(0.0))
    numerator = lax.dot_general(
        weights.astype(jnp.bfloat16),
        value_cols,
        (((1,), (1,)), ((), ())),
        preferred_element_type=jnp.float32,
    )
    return numerator, jnp.sum(weights, axis=1)


def body(
    qkv_master,
    adapter_down,
    adapter_up,
    adapter_pick,
    out_master,
    norm_gain,
    hidden_in,
    embed_in,
    prompt_len,
    prefix_len,
    prefix_holder,
    prefix_keys,
    prefix_values,
):
    chosen = adapter_pick[0]
    down_pick = lax.dynamic_index_in_dim(adapter_down, chosen, 0, keepdims=False)
    up_pick = lax.dynamic_index_in_dim(adapter_up, chosen, 0, keepdims=False).astype(jnp.bfloat16)
    joined = jnp.concatenate([hidden_in, embed_in], axis=1).astype(jnp.float32)
    factor = lax.rsqrt(jnp.mean(joined * joined, axis=1, keepdims=True) + 1e-05)
    normed = (joined * factor * norm_gain).astype(jnp.bfloat16)
    d_half = hidden_in.shape[1]

    sa, sb = pack(qkv_master, out_master, down_pick)
    ra, rb, xa, xb, gk, gv = exchange(
        sa, sb, normed[:, :d_half], normed[:, d_half:], prefix_keys[0].T, prefix_values[0].T
    )
    rows, cols = qkv_master.shape[0], up_pick.shape[1]
    out_rows = out_master.shape[0]
    head_size = cols // 3
    down_full = rb[:, :rows].reshape(128 * rows, -1)
    delta = jnp.dot(down_full, up_pick, preferred_element_type=jnp.float32)
    server_qkv = (ra.reshape(128 * rows, -1)[:, :cols].astype(jnp.float32) + delta).astype(
        jnp.bfloat16
    )
    server_out = jnp.concatenate(
        [rb[:, rows : rows + out_rows, :], ra[:, :out_rows, cols:]], axis=2
    ).reshape(128 * out_rows, head_size)
    all_rows = jnp.concatenate([xa.reshape(512, -1), xb.reshape(512, -1)], axis=1)
    qkv_rows = jnp.dot(all_rows, server_qkv, preferred_element_type=jnp.float32).astype(
        jnp.bfloat16
    )
    token_count = qkv_rows.shape[0]
    queries = qkv_rows[:, :head_size]
    new_keys = qkv_rows[:, head_size : 2 * head_size]
    new_values = qkv_rows[:, 2 * head_size :]
    inv_scale = 1.0 / math.sqrt(head_size)
    positions = jnp.arange(token_count, dtype=jnp.int32)
    lengths = prompt_len[0]
    request = (positions >= lengths[0]).astype(jnp.int32)
    allowed = (request[:, None] == request[None, :]) & (positions[None, :] <= positions[:, None])
    numerator, weight_sum = partial_attention(
        queries, new_keys.T, new_values.T, allowed, inv_scale
    )
    cached_len = prefix_len[0]
    holders = prefix_holder[0]
    slot_ids = jnp.arange(prefix_keys.shape[1], dtype=jnp.int32)
    for member in range(2):
        key_cols = lax.dynamic_index_in_dim(gk, holders[member], 0, keepdims=False)
        value_cols = lax.dynamic_index_in_dim(gv, holders[member], 0, keepdims=False)
        usable = (request == member)[:, None] & (slot_ids[None, :] < cached_len[member])
        part_num, part_sum = partial_attention(queries, key_cols, value_cols, usable, inv_scale)
        numerator = numerator + part_num
        weight_sum = weight_sum + part_sum
    attention = (numerator / weight_sum[:, None]).astype(jnp.bfloat16)
    block_out = project(attention, server_out)
    return (server_qkv, server_out, block_out, new_keys, new_values)


def solution(mesh):
    in_specs = (
        P(("dp", "tensor"), None),
        P(None, ("dp", "tensor"), None),
        P(None, None, "tensor"),
        P(),
        P(("dp", "tensor"), None),
        P(),
        P(("dp", "tensor"), None),
        P(("dp", "tensor"), None),
        P("dp", None),
        P("dp", None),
        P("dp", None),
        P("dp", None, "tensor"),
        P("dp", None, "tensor"),
    )
    out_specs = (
        P(None, "tensor"),
        P(None, "tensor"),
        P(("dp", "tensor"), None),
        P("dp", "tensor"),
        P("dp", "tensor"),
    )
    return jax.shard_map(body, mesh=mesh, in_specs=in_specs, out_specs=out_specs, check_vma=False)
```

time: 746 us -> 233 us (0.31)
  waiting for transfers between devices: 391 us -> 0 us
  blocking collectives: 206 us -> 0 us
  Pallas kernels: 0 us -> 175 us
  local copies, waits for them, and re-layouts: 73 us -> 27 us
  starting transfers between devices: 20 us -> 0 us
  matrix products: 32.2 us -> 20.9 us
  between operations: 14.7 us -> 5.52 us
    all_gather x2 -> x0, blocking collectives: 206 us -> none  [the longest x1 195 us: body(): key_piece = lax.all_gather(prefix_keys, 'dp', axis=0, tiled=True)]
    all_gather x4 -> x0, waiting for transfers between devices: 205 us -> none  [the longest x1 97.9 us: body(): lax.all_gather(merged_qkv, 'dp', axis=0, tiled=True)]
    reduce_scatter x1 -> x0, waiting for transfers between devices: 186 us -> none  [body(): lax.psum_scatter(lax.dot_general(attention, server_out, (((1,), (1,)), ((...]
    pallas_call x0 -> x3, Pallas kernels: none -> 175 us  [the longest x1 116 us: exchange(): pl.pallas_call(exchange_kernel, in_specs=[any_spec] * 6, out_specs=[any_s...]
    all_to_all x5 -> x0, local copies, waits for them, and re-layouts: 39.1 us -> none  [the longest x2 32.5 us: body(): lax.all_to_all(rows_qkv, 'tensor', split_axis=1, concat_axis=0, tiled=True)]
    all_to_all x2 -> x0, starting transfers between devices: 19.8 us -> none  [the longest x1 10.4 us: body(): lax.all_to_all(rows_qkv, 'tensor', split_axis=1, concat_axis=0, tiled=True)]
    transpose x2 -> x0, local copies, waits for them, and re-layouts: 12.2 us -> none  [regroup_rows(): jnp.transpose(shaped, (1, 0, 2, 3))]
    dot_general x11 -> x7, matrix products: 18.6 us -> 10.4 us  [the longest x1 5.39 us: body(): delta = jnp.dot(down_full, up_pick, preferred_element_type=jnp.float32)]
  transfers between devices with their start and end apart: 7 -> 0, of which waited for: 4 -> 0; matrix products, arithmetic and copies ran while one was open for 8% -> 0% of each run, Pallas kernels for 0% -> 0%
where the time goes in v1:
time: 233 us; the launch traced here: 232 us
  Pallas kernels  175 us (75%)
  local copies, waits for them, and re-layouts  27 us (12%)
  matrix products  20.9 us (9%)
  between operations  5.52 us (2%)
  other arithmetic  3.57 us (2%)
    pallas_call x1, Pallas kernels, exchange(): pl.pallas_call(exchange_kernel, in_specs=[any_spec] * 6, out_specs=[any_s...  116 us
    pallas_call x1, Pallas kernels, project(): pl.pallas_call(project_kernel, in_specs=[vmem] * 2, out_specs=vmem, out_s...  52.1 us
    unnamed x29, local copies, waits for them, and re-layouts  16.9 us
    dot_general x1, matrix products, body(): jnp.dot(all_rows, server_qkv, preferred_element_type=jnp.float32)  10.5 us
    pallas_call x1, Pallas kernels, pack(): pl.pallas_call(pack_kernel, grid=(n,), in_specs=[pl.BlockSpec((rows, mast...  7.07 us
    dot_general x1, matrix products, body(): delta = jnp.dot(down_full, up_pick, preferred_element_type=jnp.float32)  5.39 us

profile of v1, /device:TPU:0, one launch (start us, length us, event | category | flops | bytes accessed | tf_op | source)
XLA Modules:
  0.0 232.3 jit_solution(17108094667103840131)
XLA Ops:
  0.6 0.0 copy-start
  0.6 0.0 copy-start.5
  0.7 0.0 copy-start.4
  0.7 0.0 copy-start.7
  1.4 0.3 copy-done
  1.6 0.6 dynamic-slice_bitcast_fusion.down_ref
  2.3 7.1 %shard_map.164 = (bf16[32,56,768]{2,1,0:T(8,128)(2,1)}, bf16[32,88,128]{2,1,0:T(8,128)(2,1)}) custom-call(f32[56,21504]{1,0:T(8,128)} %master_ref.1, f32[28,7168]{1,0:T(8,128)} %out_ref.1, f32[56,128]{1,0:T(8,128)} %dynamic-slice_bitcast_fusion.down_ref), custom_call_target="tpu_custom_call" | custom-call | tf_op jit(solution)/shard_map/pallas_call | solution.py:49
  9.3 0.0 copy-done.5
  9.3 0.0 copy-done.4
  9.3 0.2 fusion.20
  9.5 0.0 copy-done.7
  9.5 0.1 fusion.22
  9.7 0.7 fusion.46
  10.4 116.2 %exchange.1 = (bf16[128,56,768]{2,1,0:T(8,128)(2,1)}, bf16[128,88,128]{2,1,0:T(8,128)(2,1)}, bf16[8,4,16,3584]{3,2,1,0:T(8,128)(2,1)}, bf16[8,4,16,3584]{3,2,1,0...) custom-call(bf16[32,56,768]{2,1,0:T(8,128)(2,1)} %get-tuple-element.13.sa, ...), custom_call_target="tpu_custom_call" | custom-call | tf_op jit(solution)/shard_map/exchange/pallas_call | solution.py:271
  126.6 13.4 %copy.33 = bf16[7168,672]{0,1:T(8,128)(2,1)} copy(bf16[7168,672]{1,0:T(8,128)(2,1)} %bitcast.49) | data formatting | bytes 19267584
  140.0 1.7 slice.52
  141.6 5.4 %add_convert_fusion = bf16[7168,672]{0,1:T(8,128)(2,1)S(1)} fusion(bf16[7168,672]{0,1:T(8,128)(2,1)} %copy.33, bf16[7168,128]{1,0:T(8,128)(2,1)S(1)} %bitcast.50, f32[13,128,672]{1,2,0:T(8,128)} %param.15, s32[]{:T(128)S(6)} %select_n.25), kind=kOutput, calls=%fused_computation | convolution fusion | flops 1247576064 | bytes 21274628 | tf_op jit(solution)/shard_map/dot_general | solution.py:455
  147.0 0.0 copy-start.2
  147.0 0.0 copy-start.8
  147.1 0.0 copy-start.9
  147.1 0.0 copy-start.10
  147.1 0.0 copy-start.11
  147.1 10.5 %fusion.10 = bf16[512,672]{0,1:T(8,128)(2,1)S(1)} fusion(bf16[7168,672]{0,1:T(8,128)(2,1)S(1)} %add_convert_fusion, bf16[512,3584]{1,0:T(8,128)(2,1)} %bitcast.56, bf16[512,3584]{1,0:T(8,128)(2,1)} %bitcast.55), kind=kOutput, calls=%fused_computation.15 | convolution fusion | flops 4947525632 | bytes 17661952 | tf_op jit(solution)/shard_map/dot_general | solution.py:463
  157.6 0.0 copy-done.2
  157.6 0.0 copy-done.8
  157.6 0.6 fusion.47
  160.1 0.0 copy-done.9
  160.1 0.6 fusion.48
  160.7 0.0 copy-done.10
  160.7 0.7 iota_compare_fusion.1
  161.4 0.0 copy-done.11
  161.4 1.3 fusion.49
  164.6 0.7 iota_compare_fusion.2
  165.3 0.5 fusion.51
  165.8 0.0 copy-start.12
  165.9 0.0 copy-start.3
  165.9 0.0 copy-start.6
  165.9 0.4 fusion.50
  166.3 0.3 fusion.18
  166.6 1.2 convolution_add_fusion.1
  167.9 0.2 copy.29
  168.1 0.0 copy-done.12
  168.1 1.3 fusion.14.attn
  169.4 0.0 copy-done.3
  169.4 0.0 copy-done.6
  169.4 1.3 slice.53
  170.7 1.6 slice.54
  172.3 0.0 copy-start.1
  172.3 1.9 pad_maximum_fusion
  174.3 2.8 %reshape.81.weights = bf16[3584,224]{1,0:T(8,128)(2,1)S(1)} reshape(bf16[128,28,224]{2,1,0:T(8,128)(2,1)} %pad_maximum_fusion) | data formatting | bytes 3211264 | tf_op jit(solution)/shard_map/reshape | solution.py:461
  177.1 52.1 %project.1 = bf16[16,3584]{1,0:T(8,128)(2,1)S(1)} custom-call(bf16[512,224]{1,0:T(8,128)(2,1)S(1)} %fusion.14.attn, bf16[3584,224]{1,0:T(8,128)(2,1)S(1)} %reshape.81.weights), custom_call_target="tpu_custom_call" | custom-call | tf_op jit(solution)/shard_map/project/pallas_call | solution.py:390
  229.2 2.5 %copy.31 = bf16[3584,224]{0,1:T(8,128)(2,1)} copy(bf16[3584,224]{1,0:T(8,128)(2,1)S(1)} %reshape.81.weights) | data formatting | bytes 3211264
  231.7 0.6 copy.36
  232.3 0.0 copy-done.1
  (4 shorter events, 0.1 us)
Async XLA Ops:
  0.6 1.0 copy-start
  0.6 8.7 %copy-start.5 = (bf16[16,3584]{1,0:T(8,128)(2,1)S(1)}, bf16[16,3584]{1,0:T(8,128)(2,1)}, u32[]{:S(2)}) copy-start(bf16[16,3584]{1,0:T(8,128)(2,1)} %param.19) | copy-start | bytes 344068
  0.7 8.7 %copy-start.4 = (bf16[16,3584]{1,0:T(8,128)(2,1)S(1)}, bf16[16,3584]{1,0:T(8,128)(2,1)}, u32[]{:S(2)}) copy-start(bf16[16,3584]{1,0:T(8,128)(2,1)} %param.20) | copy-start | bytes 344068
  0.7 8.9 %copy-start.7 = (f32[7168]{0:T(1024)S(1)}, f32[7168]{0:T(1024)}, u32[]{:S(2)}) copy-start(f32[7168]{0:T(1024)} %param.18) | copy-start | bytes 86020
  147.0 10.5 %copy-start.2 = (bf16[7168,672]{0,1:T(8,128)(2,1)}, bf16[7168,672]{0,1:T(8,128)(2,1)S(1)}, u32[]{:S(2)}) copy-start(bf16[7168,672]{0,1:T(8,128)(2,1)S(1)} %add_convert_fusion) | copy-start | bytes 28901380
  147.0 10.5 %copy-start.8 = (s32[1,2]{1,0:T(1,128)S(1)}, s32[1,2]{1,0:T(1,128)}, u32[]{:S(2)}) copy-start(s32[1,2]{1,0:T(1,128)} %param.23) | copy-start | bytes 28
  147.1 13.0 %copy-start.9 = (s32[1,2]{1,0:T(1,128)S(1)}, s32[1,2]{1,0:T(1,128)}, u32[]{:S(2)}) copy-start(s32[1,2]{1,0:T(1,128)} %param.22) | copy-start | bytes 28
  147.1 13.6 %copy-start.10 = (s32[1,2]{1,0:T(1,128)S(1)}, s32[1,2]{1,0:T(1,128)}, u32[]{:S(2)}) copy-start(s32[1,2]{1,0:T(1,128)} %param.21) | copy-start | bytes 28
  147.1 14.3 %copy-start.11 = (bf16[4,224,512]{2,1,0:T(8,128)(2,1)S(1)}, bf16[4,224,512]{2,1,0:T(8,128)(2,1)}, u32[]{:S(2)}) copy-start(bf16[4,224,512]{2,1,0:T(8,128)(2,1)} %get-tuple-element.19) | copy-start | bytes 2752516
  165.8 2.3 copy-start.12
  165.9 3.5 %copy-start.3 = (bf16[512,224]{0,1:T(8,128)(2,1)}, bf16[512,224]{0,1:T(8,128)(2,1)S(1)}, u32[]{:S(2)}) copy-start(bf16[512,224]{0,1:T(8,128)(2,1)S(1)} %get-tuple-element.69) | copy-start | bytes 688132
  165.9 3.5 %copy-start.6 = (bf16[512,224]{0,1:T(8,128)(2,1)}, bf16[512,224]{0,1:T(8,128)(2,1)S(1)}, u32[]{:S(2)}) copy-start(bf16[512,224]{0,1:T(8,128)(2,1)S(1)} %get-tuple-element.68) | copy-start | bytes 688132
  172.3 60.0 %copy-start.1 = (f32[13,56,128]{2,1,0:T(8,128)S(1)}, f32[13,56,128]{2,1,0:T(8,128)}, u32[]{:S(2)}) copy-start(f32[13,56,128]{2,1,0:T(8,128)} %param.14) | copy-start | bytes 1118212
